TPU v7x, 32 devices: a whole 2x2x4 slice. The times are simulated.
32 devices in a mesh: sec: 8 (over z, y), tile: 4 (over x, core).
Axes of the slice: x: 2, y: 2, z: 4, core: 2. Of those that a mesh axis runs over, the one named last changes fastest.
Arguments:
- patches: bfloat16 [48, 8, 8, 128, 128], P('sec', 'tile'), may hold values from -6 to 6
- pair_flags: int32 [48, 3], P('sec'), may hold values 0 or 1
- nodes: float32 [2, 48, 8, 8], P(None, 'sec', 'tile'), may hold values from -6 to 6
Outputs:
- relaxed: float32 [2, 48, 8, 8], P(None, 'sec', 'tile')
- measured: float32 [2, 48, 3, 8, 8], P(None, 'sec', None, 'tile')
Inputs may be any that keep to these rules, and one draw needn't show every extreme that they name: `pair_flags`: flags of pairs whose partner lies past the last section are ignored.
All inputs are finite; a program needn't handle non-finite values. No bound on the sum of `pair_flags` on one device may be relied on, other than what follows from the above.
Results may differ from a plain program's by a relative error of at most 0.0081.
Values may be sent and summed in bfloat16 or wider, within the bound.
A program may use at most 128 MiB of HBM per device.

v0:
```python
import functools
import math

import jax
import jax.numpy as jnp
import numpy as np
from jax import lax
from jax.experimental import pallas as pl
from jax.experimental.pallas import tpu as pltpu
from jax.sharding import PartitionSpec as P

SWEEPS = 8
STEP_SIZE = 0.08
EPSILON = 1e-06
LANES = 128
TILE = 8
MESH = pl.DeviceIdType.MESH


def tables(n):
    h = n // 2
    k = np.arange(n)
    phase = (k[:, None] * k[None, :] % n) * (2.0 * math.pi / n)
    c = np.asarray(np.cos(phase), np.float32).astype(jnp.bfloat16).astype(np.float32)
    s = np.asarray(np.sin(phase), np.float32).astype(jnp.bfloat16).astype(np.float32)
    part = h + TILE
    first = np.zeros((2 * part, 2 * n), np.float32)
    first[: h + 1, :n] = c[: h + 1]
    first[part : part + h, :n] = s[:h]
    second = np.concatenate([np.concatenate([c, -s], 1), np.concatenate([-s, -c], 1)], 0)
    inverse = np.concatenate([np.concatenate([c, s], 1), np.concatenate([-s, c], 1)], 0)
    order = (np.arange(n) - h) % n
    last = np.zeros((n, 2 * n), np.float32)
    last[:, 0] = c[order, 0]
    last[:, 1:h] = 2.0 * c[order, 1:h]
    last[:, h] = c[order, h]
    last[:, h + 1 : n] = -2.0 * s[order, 1:h]
    last *= 1.0 / float(n) ** 3
    return np.concatenate([first, second, inverse, last], 0).astype(jnp.bfloat16)


def open_tables(tab, n):
    part = n // 2 + TILE
    first = tab[: 2 * part, :n]
    second = tab[2 * part : 2 * part + 2 * n]
    inverse = tab[2 * part + 2 * n : 2 * part + 4 * n]
    last = tab[2 * part + 4 * n :, :n]
    return (first, second), (inverse, last)


def spectra(x, first, second, put):
    cols, n = x.shape[0], x.shape[-1]
    part = n // 2 + TILE
    lines = []
    for c in range(0, cols, 2):
        y = jnp.dot(
            first, jnp.concatenate([x[c], x[c + 1]], axis=1), preferred_element_type=jnp.float32
        )
        for d in (0, 1):
            mine = y[:, d * n : (d + 1) * n]
            lines.append(jnp.concatenate([mine[:part], mine[part:]], axis=1))
    lines = jnp.concatenate(lines, axis=0).astype(jnp.bfloat16)
    spec = jnp.dot(lines, second, preferred_element_type=jnp.float32)
    for c in range(cols):
        mine = spec[c * part : (c + 1) * part]
        put(c, mine[:, :n], mine[:, n:])


def pairs(get_a, get_b, cols, n, inverse, last, put):
    h = n // 2
    part = h + TILE
    crosses = []
    for c in range(cols):
        a, b = get_a(c), get_b(c)
        ar, ai, br, bi = a[:part], a[part:], b[:part], b[part:]
        real = ar * br + ai * bi
        imag = ar * bi - ai * br
        real_top = real[:TILE] - imag[h:]
        imag_top = imag[:TILE] + real[h:]
        real = jnp.concatenate([real_top, real[TILE:h]], axis=0).astype(jnp.bfloat16)
        imag = jnp.concatenate([imag_top, imag[TILE:h]], axis=0).astype(jnp.bfloat16)
        crosses.append(jnp.concatenate([real, imag], axis=1))
    back = jnp.dot(
        jnp.concatenate(crosses, axis=0), inverse, preferred_element_type=jnp.float32
    ).astype(jnp.bfloat16)
    place = lax.broadcasted_iota(jnp.int32, (TILE, 1), 0).astype(jnp.float32) + float(h)
    for c in range(0, cols, 2):
        sides = []
        for d in (c, c + 1):
            mine = back[d * h : (d + 1) * h]
            sides.append(jnp.concatenate([mine[:, :n], mine[:, n:]], axis=0))
        corr = jnp.dot(last, jnp.concatenate(sides, axis=1), preferred_element_type=jnp.float32)
        power = corr * corr
        total = power[:TILE]
        ramp = total
        for t in range(1, n // TILE):
            total = total + power[t * TILE : (t + 1) * TILE]
            ramp = ramp + total
        shifted = place * total - float(TILE) * ramp
        total = jnp.sum(total, axis=0, keepdims=True)
        shifted = jnp.sum(shifted, axis=0, keepdims=True)
        for d in (0, 1):
            put(c + d, shifted[:, d * n : (d + 1) * n], total[:, d * n : (d + 1) * n])


def left_share(boundary, groups, units):
    return units * (groups - 1 - boundary) // groups


def kernel(
    sizes, patches, tab_in, nodes_in, flags_in, moved, shown,
    tab, x, nodes, flags, from_right, from_left, spec, halo, stats, payload, slots, field, weight,
    tab_sem, small_sem, own_sem, left_send, left_recv, right_send, right_recv, send, recv,
):
    groups, tiles, local, reach, rows, cols, n, width = sizes
    half = LANES // 2
    part = n // 2 + TILE
    span = rows * cols
    parts = cols // width
    heap = rows * parts
    units = reach * heap
    sec = lax.axis_index("sec")
    tile = lax.axis_index("tile")
    me = sec * tiles + tile
    count = groups * tiles
    unroll = count <= 64

    def place(index):
        return (index // tiles, index % tiles)

    barrier = pltpu.get_barrier_semaphore()

    def greet(d, carry):
        pl.semaphore_signal(
            barrier, inc=1, device_id=place((me + d) % count), device_id_type=MESH
        )
        return carry

    lax.fori_loop(1, count, greet, 0, unroll=unroll)

    tab_copy = pltpu.make_async_copy(tab_in, tab, tab_sem)
    tab_copy.start()

    def own_copy(s):
        return pltpu.make_async_copy(patches.at[s], x.at[s], own_sem.at[s])

    for s in range(local):
        own_copy(s).start()
    node_copy = pltpu.make_async_copy(nodes_in, nodes, small_sem.at[0])
    flag_copy = pltpu.make_async_copy(flags_in, flags, small_sem.at[1])
    node_copy.start()
    flag_copy.start()

    has_left = (sec + groups - 1) // groups
    has_right = 1 - (sec + 1) // groups
    sent_left = has_left * left_share(sec - 1, groups, units)
    sent_right = has_right * (units - left_share(sec, groups, units))
    got_right = has_right * left_share(sec, groups, units)
    got_left = has_left * (units - left_share(sec - 1, groups, units))

    def spot(h):
        return h // parts, (h % parts) * width

    def copy_left(k):
        row, col = spot(k % heap)
        return pltpu.make_async_remote_copy(
            src_ref=patches.at[k // heap, row, pl.ds(col, width)],
            dst_ref=from_right.at[k],
            send_sem=left_send.at[k],
            recv_sem=left_recv.at[k],
            device_id=(sec - 1, tile),
            device_id_type=MESH,
        )

    def copy_right(k):
        row, col = spot(heap - 1 - k % heap)
        return pltpu.make_async_remote_copy(
            src_ref=patches.at[local - 1 - k // heap, row, pl.ds(col, width)],
            dst_ref=from_left.at[k],
            send_sem=right_send.at[k],
            recv_sem=right_recv.at[k],
            device_id=(sec + 1, tile),
            device_id_type=MESH,
        )

    stats[...] = jnp.zeros_like(stats)
    payload[...] = jnp.zeros_like(payload)
    pl.semaphore_wait(barrier, count - 1)

    def launch(k, carry):
        @pl.when(k < sent_left)
        def _():
            copy_left(k).start()

        @pl.when(k < sent_right)
        def _():
            copy_right(k).start()

        return carry

    lax.fori_loop(0, units, launch, 0)

    tab_copy.wait()
    forward, inverse = open_tables(tab, n)

    def keep(index, offset, base):
        def put(c, shifted, total):
            at = (offset - 1) * span + base + c
            stats[index, pl.ds(at, 1), :] = shifted
            stats[index, pl.ds(half + at, 1), :] = total

        return put

    def own(s, carry):
        own_copy(s).wait()
        for row in range(rows):

            def put(c, real, imag):
                spec[s, row, c, :part] = real
                spec[s, row, c, part:] = imag

            spectra(x.at[s, row], *forward, put)

        def body(offset, carry):
            for row in range(rows):
                pairs(
                    lambda c: spec[s - offset, row, c],
                    lambda c: spec[s, row, c],
                    cols, n, *inverse, keep(s - offset, offset, row * cols),
                )
            return carry

        return lax.fori_loop(1, jnp.minimum(s, reach) + 1, body, carry)

    lax.fori_loop(0, local, own, 0)

    def put_halo(c, real, imag):
        halo[c, :part] = real
        halo[c, part:] = imag

    def far(k, carry):
        @pl.when(k < got_right)
        def _():
            copy_left(k).wait_recv()
            spectra(from_right.at[k], *forward, put_halo)
            b, h = k // heap, k % heap
            row, col = spot(h)

            def body(a, carry):
                pairs(
                    lambda c: spec[local - 1 - a, row, col + c],
                    lambda c: halo[c],
                    width, n, *inverse, keep(local - 1 - a, a + b + 1, h * width),
                )
                return carry

            lax.fori_loop(0, reach - b, body, 0)

        @pl.when(k < got_left)
        def _():
            copy_right(k).wait_recv()
            spectra(from_left.at[k], *forward, put_halo)
            a, h = k // heap, heap - 1 - k % heap
            row, col = spot(h)
            first = (units - got_left + heap - 1 - h) // heap

            def body(b, carry):
                pairs(
                    lambda c: halo[c],
                    lambda c: spec[b, row, col + c],
                    width, n, *inverse, keep(local + a, a + b + 1, h * width),
                )
                return carry

            lax.fori_loop(first, reach - a, body, 0)

        return carry

    lax.fori_loop(0, jnp.maximum(got_right, got_left), far, 0)

    def sent(k, carry):
        @pl.when(k < sent_left)
        def _():
            copy_left(k).wait_send()

        @pl.when(k < sent_right)
        def _():
            copy_right(k).wait_send()

        return carry

    lax.fori_loop(0, units, sent, 0)

    sub = lax.broadcasted_iota(jnp.int32, (TILE, n), 0)
    lane = lax.broadcasted_iota(jnp.int32, (TILE, n), 1)
    shift = jnp.where(lane < n // 2, lane, lane - n).astype(jnp.float32)
    weigh = jnp.where(sub == 0, 1.0, jnp.where(sub == 1, shift, 0.0))
    node_copy.wait()
    flag_copy.wait()
    area = float(n * n)
    for index in range(local + reach):
        red = lax.dot_general(
            weigh,
            stats[index],
            (((1,), (1,)), ((), ())),
            precision=lax.Precision.HIGHEST,
            preferred_element_type=jnp.float32,
        )
        above, along = red[0:1], red[1:2]
        low = lax.broadcasted_iota(jnp.int32, (1, LANES), 1) < half
        total = jnp.where(low, pltpu.roll(above, half, 1), above) / area + EPSILON
        at = index if index < local else TILE + 2 * local - 1 - index
        payload[at : at + 1] = jnp.where(low, above, along) / area / total
    for comp in range(2):
        for row in range(rows):
            at = comp * half + reach * span + row * cols
            payload[:local, at : at + cols] = nodes[comp, :, row, :]
    for v in range(reach):
        payload[local : local + 1, v * local : (v + 1) * local] = flags[v : v + 1, :].astype(jnp.float32)

    def copy(slot, peer):
        return pltpu.make_async_remote_copy(
            src_ref=payload,
            dst_ref=slots.at[slot],
            send_sem=send.at[peer],
            recv_sem=recv.at[slot],
            device_id=place(peer),
            device_id_type=MESH,
        )

    def start(d, carry):
        copy(me, (me + d) % count).start()
        return carry

    lax.fori_loop(1, count, start, 0, unroll=unroll)
    slots[me] = payload[...]

    def finish(d, carry):
        peer = (me + d) % count
        copy(peer, peer).wait_recv()
        copy(me, peer).wait_send()
        return carry

    lax.fori_loop(1, count, finish, 0, unroll=unroll)

    lane = lax.broadcasted_iota(jnp.int32, (TILE, LANES), 1)
    sub = lax.broadcasted_iota(jnp.int32, (TILE, LANES), 0)
    owner = lane % half // span
    total = groups * local
    for g in range(groups):
        flat = jnp.broadcast_to(slots[g * tiles, local : local + 1], (TILE, LANES))
        for v in range(reach):
            w = jnp.sum(jnp.where(lane == v * local + sub, flat, 0.0), axis=1, keepdims=True)
            w = jnp.broadcast_to(w, (TILE, LANES))
            w = jnp.where(g * local + sub + v + 1 < total, w, 0.0)
            weight[v, g * local : (g + 1) * local, :] = w[:local]
        blocks = []
        for t in range(tiles):
            block = slots[g * tiles + t, :TILE]
            if g < groups - 1:
                block = block + slots[(g + 1) * tiles + t, TILE:]
            blocks.append(block)
        for v in range(reach + 1):
            value = jnp.zeros((TILE, LANES), jnp.float32)
            for t in range(tiles):
                moved_to = blocks[t]
                if t != v:
                    moved_to = pltpu.roll(moved_to, (t - v) * span % LANES, 1)
                value = jnp.where(owner == t, moved_to, value)
            value = value[:local]
            if v < reach:
                value = value * weight[v, g * local : (g + 1) * local, :]
            field[v, g * local : (g + 1) * local, :] = value

    grid_rows = tiles * rows
    at = lax.broadcasted_iota(jnp.int32, (total, LANES), 1) % half
    across = at % cols
    down = at // cols
    one = lambda mask: mask.astype(jnp.float32)
    left, right = one(across > 0), one(across < cols - 1)
    up, below = one(down > 0), one(down < grid_rows - 1)

    def sweep(_, u):
        plane = (
            up * (pltpu.roll(u, cols, 1) - u)
            + below * (pltpu.roll(u, LANES - cols, 1) - u)
            + left * (pltpu.roll(u, 1, 1) - u)
            + right * (pltpu.roll(u, LANES - 1, 1) - u)
        )
        spring = jnp.zeros_like(u)
        for v in range(reach):
            o = v + 1
            r = weight[v] * (pltpu.roll(u, total - o, 0) - u) - field[v]
            spring = spring + r - pltpu.roll(r, o, 0)
        return u + STEP_SIZE * (plane + spring)

    field[reach] = lax.fori_loop(0, SWEEPS, sweep, field[reach])
    back = (LANES - tile * span) % LANES
    for v in range(reach + 1):
        mine = pltpu.roll(field[v, pl.ds(sec * local, local), :], back, 1)
        for comp in range(2):
            for row in range(rows):
                at = comp * half + row * cols
                piece = mine[:, at : at + cols]
                if v < reach:
                    shown[comp, :, v, row, :] = piece
                else:
                    moved[comp, :, row, :] = piece


def shards(patches, pair_flags, nodes):
    local, rows, cols, n = patches.shape[:4]
    reach = pair_flags.shape[1]
    groups, tiles = lax.axis_size("sec"), lax.axis_size("tile")
    part = n // 2 + TILE
    width = cols // 2
    units = reach * rows * cols // width
    tab = jnp.asarray(tables(n))
    sizes = (groups, tiles, local, reach, rows, cols, n, width)
    hbm = pl.BlockSpec(memory_space=pltpu.HBM)
    vmem = pl.BlockSpec(memory_space=pltpu.VMEM)
    dma = pltpu.SemaphoreType.DMA
    return pl.pallas_call(
        functools.partial(kernel, sizes),
        in_specs=[hbm] * 4,
        out_specs=[vmem] * 2,
        out_shape=[
            jax.ShapeDtypeStruct((2, local, rows, cols), jnp.float32),
            jax.ShapeDtypeStruct((2, local, reach, rows, cols), jnp.float32),
        ],
        scratch_shapes=[
            pltpu.VMEM(tab.shape, jnp.bfloat16),
            pltpu.VMEM((local, rows, cols, n, n), jnp.bfloat16),
            pltpu.VMEM(nodes.shape, jnp.float32),
            pltpu.VMEM((reach, local), jnp.int32),
            pltpu.VMEM((units, width, n, n), jnp.bfloat16),
            pltpu.VMEM((units, width, n, n), jnp.bfloat16),
            pltpu.VMEM((local, rows, cols, 2 * part, n), jnp.float32),
            pltpu.VMEM((width, 2 * part, n), jnp.float32),
            pltpu.VMEM((local + reach, LANES, LANES), jnp.float32),
            pltpu.VMEM((2 * TILE, LANES), jnp.float32),
            pltpu.VMEM((groups * tiles, 2 * TILE, LANES), jnp.float32),
            pltpu.VMEM((reach + 1, groups * local, LANES), jnp.float32),
            pltpu.VMEM((reach, groups * local, LANES), jnp.float32),
            dma,
            dma((2,)),
            dma((local,)),
            dma((units,)),
            dma((units,)),
            dma((units,)),
            dma((units,)),
            dma((groups * tiles,)),
            dma((groups * tiles,)),
        ],
        compiler_params=pltpu.CompilerParams(
            collective_id=0, has_side_effects=True, vmem_limit_bytes=65000000
        ),
        name="align",
    )(patches, tab, nodes, pair_flags.T)


def solution(mesh):
    placed = (P("sec", "tile", None, None, None), P("sec", None), P(None, "sec", "tile", None))
    return jax.shard_map(
        shards,
        mesh=mesh,
        in_specs=placed,
        out_specs=(P(None, "sec", "tile", None), P(None, "sec", None, "tile", None)),
        check_vma=False,
    )
```

profile of v0, /device:TPU:27, one launch (start us, length us, event | category | flops | bytes accessed | tf_op | source)
XLA Modules:
  0.0 60.9 jit_solution(11200994605666201757)
XLA Ops:
  0.6 57.5 %align.1 = (f32[2,6,2,8]{3,2,1,0:T(2,128)}, f32[2,6,3,2,8]{4,3,2,1,0:T(2,128)}) custom-call(bf16[6,2,8,128,128]{4,3,2,1,0:T(8,128)(2,1)} %patches.1, bf16[784,256]{1,0:T(8,128)(2,1)} %constant.2.clone.tab_in, f32[2,6,2,8]{3,2,1,0:T(2,128)} %nodes_in.1, s32[3,6]{1,0:T(4,128)} %bitcast.1), custom_call_target="tpu_custom_call" | custom-call | tf_op jit(solution)/shard_map/align/pallas_call | solution.py:423
  58.2 1.3 %copy.8 = f32[2,6,2,8]{3,2,1,0:T(2,128)} copy(f32[2,6,2,8]{3,2,1,0:T(2,128)} %get-tuple-element.4) | data formatting | bytes 1536
  59.5 1.4 %copy.9 = f32[2,6,3,2,8]{4,3,2,1,0:T(2,128)} copy(f32[2,6,3,2,8]{4,3,2,1,0:T(2,128)} %get-tuple-element.5) | data formatting | bytes 4608
where the time goes:
time: 61.1 us; the launch traced here: 60.9 us
  Pallas kernels  57.5 us (94%)
  local copies, waits for them, and re-layouts  2.7 us (4%)
  between operations  0.64 us (1%)
    pallas_call x1, Pallas kernels, shards(): pl.pallas_call(functools.partial(kernel, sizes), in_specs=[hbm] * 4, out_...  57.5 us
    unnamed x2, local copies, waits for them, and re-layouts  2.7 us

commit v1 on v0

--- a/solution.py
+++ b/solution.py
@@ -14,6 +14,7 @@
 EPSILON = 1e-06
 LANES = 128
 TILE = 8
+AHEAD = 4
 MESH = pl.DeviceIdType.MESH
 
 
@@ -110,7 +111,7 @@
 def kernel(
     sizes, patches, tab_in, nodes_in, flags_in, moved, shown,
     tab, x, nodes, flags, from_right, from_left, spec, halo, stats, payload, slots, field, weight,
-    tab_sem, small_sem, own_sem, left_send, left_recv, right_send, right_recv, send, recv,
+    tab_sem, small_sem, own_sem, left_send, left_recv, right_send, right_recv, send, recv, chain,
 ):
     groups, tiles, local, reach, rows, cols, n, width = sizes
     half = LANES // 2
@@ -130,13 +131,18 @@
 
     barrier = pltpu.get_barrier_semaphore()
 
-    def greet(d, carry):
+    for d in range(1, tiles):
         pl.semaphore_signal(
-            barrier, inc=1, device_id=place((me + d) % count), device_id_type=MESH
-        )
-        return carry
-
-    lax.fori_loop(1, count, greet, 0, unroll=unroll)
+            barrier, inc=1, device_id=(sec, (tile + d) % tiles), device_id_type=MESH
+        )
+
+    @pl.when(sec > 0)
+    def _():
+        pl.semaphore_signal(barrier, inc=1, device_id=(sec - 1, tile), device_id_type=MESH)
+
+    @pl.when(sec < groups - 1)
+    def _():
+        pl.semaphore_signal(barrier, inc=1, device_id=(sec + 1, tile), device_id_type=MESH)
 
     tab_copy = pltpu.make_async_copy(tab_in, tab, tab_sem)
     tab_copy.start()
@@ -185,20 +191,50 @@
 
     stats[...] = jnp.zeros_like(stats)
     payload[...] = jnp.zeros_like(payload)
-    pl.semaphore_wait(barrier, count - 1)
+    pl.semaphore_wait(barrier, tiles - 1 + has_left + has_right)
+
+    late = left_share(sec, groups, units) - 1
 
     def launch(k, carry):
         @pl.when(k < sent_left)
         def _():
             copy_left(k).start()
 
-        @pl.when(k < sent_right)
-        def _():
-            copy_right(k).start()
+        @pl.when((k >= late) & (k - late < sent_right))
+        def _():
+            copy_right(k - late).start()
 
         return carry
 
-    lax.fori_loop(0, units, launch, 0)
+    def tell():
+        @pl.when(sec > 0)
+        def _():
+            pl.semaphore_signal(chain.at[1], inc=1, device_id=(sec - 1, tile), device_id_type=MESH)
+
+        @pl.when(sec < groups - 1)
+        def _():
+            pl.semaphore_signal(chain.at[0], inc=1, device_id=(sec + 1, tile), device_id_type=MESH)
+
+    rounds = groups - 2
+
+    def relay(s, carry):
+        @pl.when((s < rounds) & (sec > 0))
+        def _():
+            pl.semaphore_wait(chain.at[0], 1)
+
+        @pl.when((s < rounds) & (sec < groups - 1))
+        def _():
+            pl.semaphore_wait(chain.at[1], 1)
+
+        @pl.when(s + 1 < rounds)
+        def _():
+            tell()
+
+        return carry
+
+    launch(0, 0)
+    if rounds > 0:
+        tell()
 
     tab_copy.wait()
     forward, inverse = open_tables(tab, n)
@@ -212,6 +248,10 @@
         return put
 
     def own(s, carry):
+        @pl.when(s > 0)
+        def _():
+            launch(s, 0)
+
         own_copy(s).wait()
         for row in range(rows):
 
@@ -230,15 +270,21 @@
                 )
             return carry
 
-        return lax.fori_loop(1, jnp.minimum(s, reach) + 1, body, carry)
+        lax.fori_loop(1, jnp.minimum(s, reach) + 1, body, 0)
+        return relay(s, carry)
 
     lax.fori_loop(0, local, own, 0)
+    lax.fori_loop(local, rounds, relay, 0)
 
     def put_halo(c, real, imag):
         halo[c, :part] = real
         halo[c, part:] = imag
 
     def far(k, carry):
+        @pl.when(k + AHEAD >= local)
+        def _():
+            launch(k + AHEAD, 0)
+
         @pl.when(k < got_right)
         def _():
             copy_left(k).wait_recv()
@@ -256,11 +302,12 @@
 
             lax.fori_loop(0, reach - b, body, 0)
 
-        @pl.when(k < got_left)
-        def _():
-            copy_right(k).wait_recv()
-            spectra(from_left.at[k], *forward, put_halo)
-            a, h = k // heap, heap - 1 - k % heap
+        @pl.when(k >= got_right)
+        def _():
+            u = k - got_right
+            copy_right(u).wait_recv()
+            spectra(from_left.at[u], *forward, put_halo)
+            a, h = u // heap, heap - 1 - u % heap
             row, col = spot(h)
             first = (units - got_left + heap - 1 - h) // heap
 
@@ -276,7 +323,9 @@
 
         return carry
 
-    lax.fori_loop(0, jnp.maximum(got_right, got_left), far, 0)
+    got = got_right + got_left
+    lax.fori_loop(0, got, far, 0)
+    lax.fori_loop(jnp.maximum(local, got + AHEAD), 2 * units, launch, 0)
 
     def sent(k, carry):
         @pl.when(k < sent_left)
@@ -451,9 +500,10 @@
             dma((units,)),
             dma((groups * tiles,)),
             dma((groups * tiles,)),
+            pltpu.SemaphoreType.REGULAR((2,)),
         ],
         compiler_params=pltpu.CompilerParams(
-            collective_id=0, has_side_effects=True, vmem_limit_bytes=65000000
+            collective_id=0, has_side_effects=True, vmem_limit_bytes=(64 << 20) - (160 << 10)
         ),
         name="align",
     )(patches, tab, nodes, pair_flags.T)

time: 61.1 us -> 52.2 us (0.85)
  the two profiles are of different devices: /device:TPU:27 before, /device:TPU:0 now
where the time goes in v1:
time: 52.2 us; the launch traced here: 51.5 us
  Pallas kernels  48.1 us (92%)
  local copies, waits for them, and re-layouts  2.7 us (5%)
  between operations  0.64 us (1%)
    pallas_call x1, Pallas kernels, shards(): pl.pallas_call(functools.partial(kernel, sizes), in_specs=[hbm] * 4, out_...  48.1 us
    unnamed x2, local copies, waits for them, and re-layouts  2.7 us

profile of v1, /device:TPU:0, one launch (start us, length us, event | category | flops | bytes accessed | tf_op | source)
XLA Modules:
  0.0 51.5 jit_solution(8213732012569986892)
XLA Ops:
  0.6 48.1 %align.1 = (f32[2,6,2,8]{3,2,1,0:T(2,128)}, f32[2,6,3,2,8]{4,3,2,1,0:T(2,128)}) custom-call(bf16[6,2,8,128,128]{4,3,2,1,0:T(8,128)(2,1)} %patches.1, bf16[784,256]{1,0:T(8,128)(2,1)} %constant.2.clone.tab_in, f32[2,6,2,8]{3,2,1,0:T(2,128)} %nodes_in.1, s32[3,6]{1,0:T(4,128)} %bitcast.1), custom_call_target="tpu_custom_call" | custom-call | tf_op jit(solution)/shard_map/align/pallas_call | solution.py:472
  48.8 1.3 %copy.8 = f32[2,6,2,8]{3,2,1,0:T(2,128)} copy(f32[2,6,2,8]{3,2,1,0:T(2,128)} %get-tuple-element.4) | data formatting | bytes 1536
  50.1 1.4 %copy.9 = f32[2,6,3,2,8]{4,3,2,1,0:T(2,128)} copy(f32[2,6,3,2,8]{4,3,2,1,0:T(2,128)} %get-tuple-element.5) | data formatting | bytes 4608

commit v2 on v1

--- a/solution.py
+++ b/solution.py
@@ -14,7 +14,6 @@
 EPSILON = 1e-06
 LANES = 128
 TILE = 8
-AHEAD = 4
 MESH = pl.DeviceIdType.MESH
 
 
@@ -124,11 +123,11 @@
     tile = lax.axis_index("tile")
     me = sec * tiles + tile
     count = groups * tiles
-    unroll = count <= 64
 
     def place(index):
         return (index // tiles, index % tiles)
 
+    slots[...] = jnp.zeros_like(slots)
     barrier = pltpu.get_barrier_semaphore()
 
     for d in range(1, tiles):
@@ -157,53 +156,62 @@
     node_copy.start()
     flag_copy.start()
 
+    halves = 2 * units
     has_left = (sec + groups - 1) // groups
     has_right = 1 - (sec + 1) // groups
-    sent_left = has_left * left_share(sec - 1, groups, units)
-    sent_right = has_right * (units - left_share(sec, groups, units))
-    got_right = has_right * left_share(sec, groups, units)
-    got_left = has_left * (units - left_share(sec - 1, groups, units))
+    near = left_share(sec, groups, halves)
+    before = left_share(sec - 1, groups, halves)
+    sent_left = has_left * ((before + 1) // 2)
+    sent_right = has_right * ((halves - near + 1) // 2)
+    got_right = has_right * ((near + 1) // 2)
+    got_left = has_left * ((halves - before + 1) // 2)
+    odd_near, odd_before = near % 2, before % 2
 
     def spot(h):
         return h // parts, (h % parts) * width
 
-    def copy_left(k):
+    def copy_left(k, size):
         row, col = spot(k % heap)
         return pltpu.make_async_remote_copy(
-            src_ref=patches.at[k // heap, row, pl.ds(col, width)],
-            dst_ref=from_right.at[k],
+            src_ref=patches.at[k // heap, row, pl.ds(col, size)],
+            dst_ref=from_right.at[k, pl.ds(0, size)],
             send_sem=left_send.at[k],
             recv_sem=left_recv.at[k],
             device_id=(sec - 1, tile),
             device_id_type=MESH,
         )
 
-    def copy_right(k):
+    def copy_right(k, size):
         row, col = spot(heap - 1 - k % heap)
+        rest = width - size
         return pltpu.make_async_remote_copy(
-            src_ref=patches.at[local - 1 - k // heap, row, pl.ds(col, width)],
-            dst_ref=from_left.at[k],
+            src_ref=patches.at[local - 1 - k // heap, row, pl.ds(col + rest, size)],
+            dst_ref=from_left.at[k, pl.ds(rest, size)],
             send_sem=right_send.at[k],
             recv_sem=right_recv.at[k],
             device_id=(sec + 1, tile),
             device_id_type=MESH,
         )
 
+    def each(copy, act, k, count, odd):
+        part_unit = (odd == 1) & (k == count - 1)
+
+        @pl.when((k >= 0) & (k < count) & jnp.logical_not(part_unit))
+        def _():
+            act(copy(k, width))
+
+        @pl.when(part_unit)
+        def _():
+            act(copy(k, width // 2))
+
     stats[...] = jnp.zeros_like(stats)
-    payload[...] = jnp.zeros_like(payload)
     pl.semaphore_wait(barrier, tiles - 1 + has_left + has_right)
 
-    late = left_share(sec, groups, units) - 1
+    begin = lambda copy: copy.start()
 
     def launch(k, carry):
-        @pl.when(k < sent_left)
-        def _():
-            copy_left(k).start()
-
-        @pl.when((k >= late) & (k - late < sent_right))
-        def _():
-            copy_right(k - late).start()
-
+        each(copy_left, begin, k, sent_left, odd_before)
+        each(copy_right, begin, k, sent_right, odd_near)
         return carry
 
     def tell():
@@ -232,15 +240,19 @@
 
         return carry
 
-    launch(0, 0)
+    lax.fori_loop(0, units, launch, 0)
     if rounds > 0:
         tell()
 
     tab_copy.wait()
     forward, inverse = open_tables(tab, n)
 
-    def keep(index, offset, base):
+    def keep(index, offset, base, low=None, high=None):
         def put(c, shifted, total):
+            valid = low if c < width // 2 else high
+            if valid is not None:
+                shifted = jnp.where(valid, shifted, 0.0)
+                total = jnp.where(valid, total, 0.0)
             at = (offset - 1) * span + base + c
             stats[index, pl.ds(at, 1), :] = shifted
             stats[index, pl.ds(half + at, 1), :] = total
@@ -248,10 +260,6 @@
         return put
 
     def own(s, carry):
-        @pl.when(s > 0)
-        def _():
-            launch(s, 0)
-
         own_copy(s).wait()
         for row in range(rows):
 
@@ -281,41 +289,42 @@
         halo[c, part:] = imag
 
     def far(k, carry):
-        @pl.when(k + AHEAD >= local)
-        def _():
-            launch(k + AHEAD, 0)
-
-        @pl.when(k < got_right)
-        def _():
-            copy_left(k).wait_recv()
+        odd = sec % 2
+        u = k - odd * got_right
+        k = k - (1 - odd) * got_left
+
+        @pl.when((k >= 0) & (k < got_right))
+        def _():
+            each(copy_left, lambda copy: copy.wait_recv(), k, got_right, odd_near)
             spectra(from_right.at[k], *forward, put_halo)
             b, h = k // heap, k % heap
             row, col = spot(h)
+            whole = (odd_near == 0) | (k < got_right - 1)
 
             def body(a, carry):
                 pairs(
                     lambda c: spec[local - 1 - a, row, col + c],
                     lambda c: halo[c],
-                    width, n, *inverse, keep(local - 1 - a, a + b + 1, h * width),
+                    width, n, *inverse, keep(local - 1 - a, a + b + 1, h * width, None, whole),
                 )
                 return carry
 
             lax.fori_loop(0, reach - b, body, 0)
 
-        @pl.when(k >= got_right)
-        def _():
-            u = k - got_right
-            copy_right(u).wait_recv()
+        @pl.when((u >= 0) & (u < got_left))
+        def _():
+            each(copy_right, lambda copy: copy.wait_recv(), u, got_left, odd_before)
             spectra(from_left.at[u], *forward, put_halo)
             a, h = u // heap, heap - 1 - u % heap
             row, col = spot(h)
-            first = (units - got_left + heap - 1 - h) // heap
+            first = (before // 2 + heap - 1 - h) // heap
 
             def body(b, carry):
+                whole = (odd_before == 0) | (b * heap + h > before // 2)
                 pairs(
                     lambda c: halo[c],
                     lambda c: spec[b, row, col + c],
-                    width, n, *inverse, keep(local + a, a + b + 1, h * width),
+                    width, n, *inverse, keep(local + a, a + b + 1, h * width, whole, None),
                 )
                 return carry
 
@@ -325,17 +334,11 @@
 
     got = got_right + got_left
     lax.fori_loop(0, got, far, 0)
-    lax.fori_loop(jnp.maximum(local, got + AHEAD), 2 * units, launch, 0)
 
     def sent(k, carry):
-        @pl.when(k < sent_left)
-        def _():
-            copy_left(k).wait_send()
-
-        @pl.when(k < sent_right)
-        def _():
-            copy_right(k).wait_send()
-
+        done = lambda copy: copy.wait_send()
+        each(copy_left, done, k, sent_left, odd_before)
+        each(copy_right, done, k, sent_right, odd_near)
         return carry
 
     lax.fori_loop(0, units, sent, 0)
@@ -358,7 +361,7 @@
         above, along = red[0:1], red[1:2]
         low = lax.broadcasted_iota(jnp.int32, (1, LANES), 1) < half
         total = jnp.where(low, pltpu.roll(above, half, 1), above) / area + EPSILON
-        at = index if index < local else TILE + 2 * local - 1 - index
+        at = index if index < local else 2 * local + reach - index
         payload[at : at + 1] = jnp.where(low, above, along) / area / total
     for comp in range(2):
         for row in range(rows):
@@ -377,20 +380,30 @@
             device_id_type=MESH,
         )
 
-    def start(d, carry):
-        copy(me, (me + d) % count).start()
-        return carry
-
-    lax.fori_loop(1, count, start, 0, unroll=unroll)
+    span_of = 2 * min(groups - 1, -(-SWEEPS * reach // local)) + 1
+    others = span_of * tiles
+
+    def peers(act):
+        def visit(d, carry):
+            to = sec + d // tiles - span_of // 2
+            peer = to * tiles + d % tiles
+
+            @pl.when((to >= 0) & (to < groups) & (peer != me))
+            def _():
+                act(peer)
+
+            return carry
+
+        lax.fori_loop(0, others, visit, 0, unroll=others <= 64)
+
+    peers(lambda peer: copy(me, peer).start())
     slots[me] = payload[...]
 
-    def finish(d, carry):
-        peer = (me + d) % count
+    def finish(peer):
         copy(peer, peer).wait_recv()
         copy(me, peer).wait_send()
-        return carry
-
-    lax.fori_loop(1, count, finish, 0, unroll=unroll)
+
+    peers(finish)
 
     lane = lax.broadcasted_iota(jnp.int32, (TILE, LANES), 1)
     sub = lax.broadcasted_iota(jnp.int32, (TILE, LANES), 0)
@@ -405,10 +418,11 @@
             weight[v, g * local : (g + 1) * local, :] = w[:local]
         blocks = []
         for t in range(tiles):
-            block = slots[g * tiles + t, :TILE]
+            block = slots[g * tiles + t, :local]
             if g < groups - 1:
-                block = block + slots[(g + 1) * tiles + t, TILE:]
-            blocks.append(block)
+                add = slots[(g + 1) * tiles + t, local + 1 :]
+                block = jnp.concatenate([block[: local - reach], block[local - reach :] + add], axis=0)
+            blocks.append(jnp.concatenate([block, jnp.zeros((TILE - local, LANES), jnp.float32)], axis=0))
         for v in range(reach + 1):
             value = jnp.zeros((TILE, LANES), jnp.float32)
             for t in range(tiles):
@@ -487,8 +501,8 @@
             pltpu.VMEM((local, rows, cols, 2 * part, n), jnp.float32),
             pltpu.VMEM((width, 2 * part, n), jnp.float32),
             pltpu.VMEM((local + reach, LANES, LANES), jnp.float32),
-            pltpu.VMEM((2 * TILE, LANES), jnp.float32),
-            pltpu.VMEM((groups * tiles, 2 * TILE, LANES), jnp.float32),
+            pltpu.VMEM((local + reach + 1, LANES), jnp.float32),
+            pltpu.VMEM((groups * tiles, local + reach + 1, LANES), jnp.float32),
             pltpu.VMEM((reach + 1, groups * local, LANES), jnp.float32),
             pltpu.VMEM((reach, groups * local, LANES), jnp.float32),
             dma,
@@ -503,10 +517,10 @@
             pltpu.SemaphoreType.REGULAR((2,)),
         ],
         compiler_params=pltpu.CompilerParams(
-            collective_id=0, has_side_effects=True, vmem_limit_bytes=(64 << 20) - (160 << 10)
+            collective_id=0, has_side_effects=True, vmem_limit_bytes=48 << 20
         ),
         name="align",
-    )(patches, tab, nodes, pair_flags.T)
+    )(*[pltpu.with_memory_space_constraint(a, pltpu.HBM) for a in (patches, tab, nodes, pair_flags.T)])
 
 
 def solution(mesh):

time: 52.2 us -> 46.9 us (0.90); the launches traced: 51.5 us -> 46.8 us
  Pallas kernels: 48.1 us -> 44.9 us
  local copies, waits for them, and re-layouts: 2.7 us -> 1.22 us
    pallas_call x1, Pallas kernels: 48.1 us -> 44.9 us  [shards(): pl.pallas_call(functools.partial(kernel, sizes), in_specs=[hbm] * 4, out_...]
    unnamed x2, local copies, waits for them, and re-layouts: 2.7 us -> 1.22 us
where the time goes in v2:
time: 46.9 us; the launch traced here: 46.8 us
  Pallas kernels  44.9 us (96%)
  local copies, waits for them, and re-layouts  1.22 us (3%)
  between operations  0.64 us (1%)
    pallas_call x1, Pallas kernels, shards(): pl.pallas_call(functools.partial(kernel, sizes), in_specs=[hbm] * 4, out_...  44.9 us
    unnamed x2, local copies, waits for them, and re-layouts  1.22 us

profile of v2, /device:TPU:0, one launch (start us, length us, event | category | flops | bytes accessed | tf_op | source)
XLA Modules:
  0.0 46.8 jit_solution(4209598994360754122)
XLA Ops:
  0.6 44.9 %align.1 = (f32[2,6,2,8]{3,2,1,0:T(2,128)S(1)}, f32[2,6,3,2,8]{4,3,2,1,0:T(2,128)S(1)}) custom-call(bf16[6,2,8,128,128]{4,3,2,1,0:T(8,128)(2,1)} %patches.1, bf16[784,256]{1,0:T(8,128)(2,1)} %constant.2.clone.tab_in, f32[2,6,2,8]{3,2,1,0:T(2,128)} %nodes_in.1, s32[3,6]{1,0:T(4,128)} %bitcast.1), custom_call_target="tpu_custom_call" | custom-call | tf_op jit(solution)/shard_map/align/pallas_call | solution.py:486
  45.5 0.6 %copy.8 = f32[2,6,2,8]{3,2,1,0:T(2,128)} copy(f32[2,6,2,8]{3,2,1,0:T(2,128)S(1)} %get-tuple-element.4) | data formatting | bytes 1536
  46.1 0.6 %copy.9 = f32[2,6,3,2,8]{4,3,2,1,0:T(2,128)} copy(f32[2,6,3,2,8]{4,3,2,1,0:T(2,128)S(1)} %get-tuple-element.5) | data formatting | bytes 4608

commit v3 on v2

--- a/solution.py
+++ b/solution.py
@@ -107,12 +107,45 @@
     return units * (groups - 1 - boundary) // groups
 
 
+def late_cells(groups, local, reach, heap, window):
+    units = reach * heap
+    halves = 2 * units
+    cells = []
+    for g in range(groups):
+        near = left_share(g, groups, halves) if g < groups - 1 else 0
+        before = left_share(g - 1, groups, halves) if g else halves
+        right = [("right", k) for k in range((near + 1) // 2)]
+        left = [("left", k) for k in range((halves - before + 1) // 2)]
+        order = (right + left) if g % 2 else (left + right)
+        mine = {}
+        for side, k in order[-window:]:
+            if side == "right":
+                b, h = k // heap, k % heap
+                items = [(a, b) for a in range(reach - b)]
+            else:
+                a, h = k // heap, heap - 1 - k % heap
+                items = [(a, b) for b in range((before // 2 + heap - 1 - h) // heap, reach - a)]
+            for a, b in items:
+                section = (g if side == "right" else g - 1) * local + local - 1 - a
+                for part in (0, 1):
+                    cut = near if side == "right" else before
+                    if cut % 2 and b * heap + h == cut // 2 and part == (side == "right"):
+                        continue
+                    key = (a + b, 2 * h + part)
+                    if key in mine:
+                        return None
+                    mine[key] = section
+        cells.append(mine)
+    return cells
+
+
 def kernel(
     sizes, patches, tab_in, nodes_in, flags_in, moved, shown,
-    tab, x, nodes, flags, from_right, from_left, spec, halo, stats, payload, slots, field, weight,
+    tab, x, nodes, flags, from_right, from_left, spec, halo, stats, slots, late, lates, field, weight,
     tab_sem, small_sem, own_sem, left_send, left_recv, right_send, right_recv, send, recv, chain,
+    pair_sem, even_send, even_recv, tile_send, tile_recv,
 ):
-    groups, tiles, local, reach, rows, cols, n, width = sizes
+    groups, tiles, local, reach, rows, cols, n, width, window, cells = sizes
     half = LANES // 2
     part = n // 2 + TILE
     span = rows * cols
@@ -127,7 +160,7 @@
     def place(index):
         return (index // tiles, index % tiles)
 
-    slots[...] = jnp.zeros_like(slots)
+    lates[...] = jnp.zeros_like(lates)
     barrier = pltpu.get_barrier_semaphore()
 
     for d in range(1, tiles):
@@ -193,10 +226,10 @@
             device_id_type=MESH,
         )
 
-    def each(copy, act, k, count, odd):
-        part_unit = (odd == 1) & (k == count - 1)
-
-        @pl.when((k >= 0) & (k < count) & jnp.logical_not(part_unit))
+    def each(copy, act, k, count, odd, also=True):
+        part_unit = (odd == 1) & (k == count - 1) & also
+
+        @pl.when((k >= 0) & (k < count - odd) & also)
         def _():
             act(copy(k, width))
 
@@ -208,10 +241,18 @@
     pl.semaphore_wait(barrier, tiles - 1 + has_left + has_right)
 
     begin = lambda copy: copy.start()
+    odd_sec = sec % 2
+    hold_left = 2 * odd_sec
+    hold_right = 2 - hold_left
 
     def launch(k, carry):
-        each(copy_left, begin, k, sent_left, odd_before)
-        each(copy_right, begin, k, sent_right, odd_near)
+        each(copy_left, begin, k, sent_left, odd_before, k < sent_left - hold_left)
+        each(copy_right, begin, k, sent_right, odd_near, k < sent_right - hold_right)
+        return carry
+
+    def launch_held(k, carry):
+        each(copy_left, begin, k, sent_left, odd_before, k >= sent_left - hold_left)
+        each(copy_right, begin, k, sent_right, odd_near, k >= sent_right - hold_right)
         return carry
 
     def tell():
@@ -247,7 +288,9 @@
     tab_copy.wait()
     forward, inverse = open_tables(tab, n)
 
-    def keep(index, offset, base, low=None, high=None):
+    def keep(index, offset, base, low=None, high=None, fresh=False):
+        index = jnp.where(fresh, local + reach, index)
+
         def put(c, shifted, total):
             valid = low if c < width // 2 else high
             if valid is not None:
@@ -284,73 +327,14 @@
     lax.fori_loop(0, local, own, 0)
     lax.fori_loop(local, rounds, relay, 0)
 
-    def put_halo(c, real, imag):
-        halo[c, :part] = real
-        halo[c, part:] = imag
-
-    def far(k, carry):
-        odd = sec % 2
-        u = k - odd * got_right
-        k = k - (1 - odd) * got_left
-
-        @pl.when((k >= 0) & (k < got_right))
-        def _():
-            each(copy_left, lambda copy: copy.wait_recv(), k, got_right, odd_near)
-            spectra(from_right.at[k], *forward, put_halo)
-            b, h = k // heap, k % heap
-            row, col = spot(h)
-            whole = (odd_near == 0) | (k < got_right - 1)
-
-            def body(a, carry):
-                pairs(
-                    lambda c: spec[local - 1 - a, row, col + c],
-                    lambda c: halo[c],
-                    width, n, *inverse, keep(local - 1 - a, a + b + 1, h * width, None, whole),
-                )
-                return carry
-
-            lax.fori_loop(0, reach - b, body, 0)
-
-        @pl.when((u >= 0) & (u < got_left))
-        def _():
-            each(copy_right, lambda copy: copy.wait_recv(), u, got_left, odd_before)
-            spectra(from_left.at[u], *forward, put_halo)
-            a, h = u // heap, heap - 1 - u % heap
-            row, col = spot(h)
-            first = (before // 2 + heap - 1 - h) // heap
-
-            def body(b, carry):
-                whole = (odd_before == 0) | (b * heap + h > before // 2)
-                pairs(
-                    lambda c: halo[c],
-                    lambda c: spec[b, row, col + c],
-                    width, n, *inverse, keep(local + a, a + b + 1, h * width, whole, None),
-                )
-                return carry
-
-            lax.fori_loop(first, reach - a, body, 0)
-
-        return carry
-
-    got = got_right + got_left
-    lax.fori_loop(0, got, far, 0)
-
-    def sent(k, carry):
-        done = lambda copy: copy.wait_send()
-        each(copy_left, done, k, sent_left, odd_before)
-        each(copy_right, done, k, sent_right, odd_near)
-        return carry
-
-    lax.fori_loop(0, units, sent, 0)
-
-    sub = lax.broadcasted_iota(jnp.int32, (TILE, n), 0)
-    lane = lax.broadcasted_iota(jnp.int32, (TILE, n), 1)
-    shift = jnp.where(lane < n // 2, lane, lane - n).astype(jnp.float32)
-    weigh = jnp.where(sub == 0, 1.0, jnp.where(sub == 1, shift, 0.0))
-    node_copy.wait()
-    flag_copy.wait()
     area = float(n * n)
-    for index in range(local + reach):
+    mine = tile * groups + sec
+
+    def ratios(index):
+        sub = lax.broadcasted_iota(jnp.int32, (TILE, n), 0)
+        lane = lax.broadcasted_iota(jnp.int32, (TILE, n), 1)
+        shift = jnp.where(lane < n // 2, lane, lane - n).astype(jnp.float32)
+        weigh = jnp.where(sub == 0, 1.0, jnp.where(sub == 1, shift, 0.0))
         red = lax.dot_general(
             weigh,
             stats[index],
@@ -361,21 +345,148 @@
         above, along = red[0:1], red[1:2]
         low = lax.broadcasted_iota(jnp.int32, (1, LANES), 1) < half
         total = jnp.where(low, pltpu.roll(above, half, 1), above) / area + EPSILON
-        at = index if index < local else 2 * local + reach - index
-        payload[at : at + 1] = jnp.where(low, above, along) / area / total
-    for comp in range(2):
-        for row in range(rows):
-            at = comp * half + reach * span + row * cols
-            payload[:local, at : at + cols] = nodes[comp, :, row, :]
-    for v in range(reach):
-        payload[local : local + 1, v * local : (v + 1) * local] = flags[v : v + 1, :].astype(jnp.float32)
-
-    def copy(slot, peer):
+        return jnp.where(low, above, along) / area / total
+
+    def pair_copy():
         return pltpu.make_async_remote_copy(
-            src_ref=payload,
-            dst_ref=slots.at[slot],
+            src_ref=slots.at[mine],
+            dst_ref=slots.at[mine],
+            send_sem=pair_sem.at[0],
+            recv_sem=pair_sem.at[1],
+            device_id=(sec + 1 - 2 * odd_sec, tile),
+            device_id_type=MESH,
+        )
+
+    def even_copy(pair, other):
+        both = pl.ds(tile * groups + 2 * pair, 2)
+        return pltpu.make_async_remote_copy(
+            src_ref=slots.at[both],
+            dst_ref=slots.at[both],
+            send_sem=even_send.at[other],
+            recv_sem=even_recv.at[pair],
+            device_id=(2 * other + odd_sec, tile),
+            device_id_type=MESH,
+        )
+
+    def tile_copy(column, other):
+        whole = pl.ds(column * groups, groups)
+        return pltpu.make_async_remote_copy(
+            src_ref=slots.at[whole],
+            dst_ref=slots.at[whole],
+            send_sem=tile_send.at[other],
+            recv_sem=tile_recv.at[column],
+            device_id=(sec, other),
+            device_id_type=MESH,
+        )
+
+    def evens(act):
+        def visit(d, carry):
+            act((sec // 2 + d) % (groups // 2))
+            return carry
+
+        lax.fori_loop(1, groups // 2, visit, 0)
+
+    def columns(act):
+        def visit(d, carry):
+            act((tile + d) % tiles)
+            return carry
+
+        lax.fori_loop(1, tiles, visit, 0)
+
+    def publish():
+        node_copy.wait()
+        flag_copy.wait()
+        slots[mine] = jnp.zeros(slots.shape[1:], jnp.float32)
+        for index in range(local + reach):
+            at = index if index < local else 2 * local + reach - index
+            slots[mine, at : at + 1] = ratios(index)
+        for comp in range(2):
+            for row in range(rows):
+                at = comp * half + reach * span + row * cols
+                slots[mine, :local, at : at + cols] = nodes[comp, :, row, :]
+        for v in range(reach):
+            slots[mine, local : local + 1, v * local : (v + 1) * local] = flags[v : v + 1, :].astype(
+                jnp.float32
+            )
+        pair_copy().start()
+        lax.fori_loop(0, units, launch_held, 0)
+
+    def spread_pairs():
+        pair_copy().wait()
+        evens(lambda other: even_copy(sec // 2, other).start())
+
+    def spread_columns():
+        evens(lambda other: even_copy(other, other).wait_recv())
+        evens(lambda other: even_copy(sec // 2, other).wait_send())
+        columns(lambda other: tile_copy(tile, other).start())
+
+    stages = (publish, spread_pairs, spread_columns)
+
+    def put_halo(c, real, imag):
+        halo[c, :part] = real
+        halo[c, part:] = imag
+
+    got = got_right + got_left
+
+    def far(k, carry):
+        fresh = k >= got - window
+        for number, stage in enumerate(stages[:window]):
+            pl.when(k == got - window + number)(stage)
+
+        u = k - odd_sec * got_right
+        k = k - (1 - odd_sec) * got_left
+
+        @pl.when((k >= 0) & (k < got_right))
+        def _():
+            each(copy_left, lambda copy: copy.wait_recv(), k, got_right, odd_near)
+            spectra(from_right.at[k], *forward, put_halo)
+            b, h = k // heap, k % heap
+            row, col = spot(h)
+            whole = (odd_near == 0) | (k < got_right - 1)
+
+            def body(a, carry):
+                pairs(
+                    lambda c: spec[local - 1 - a, row, col + c],
+                    lambda c: halo[c],
+                    width, n, *inverse, keep(local - 1 - a, a + b + 1, h * width, None, whole, fresh),
+                )
+                return carry
+
+            lax.fori_loop(0, reach - b, body, 0)
+
+        @pl.when((u >= 0) & (u < got_left))
+        def _():
+            each(copy_right, lambda copy: copy.wait_recv(), u, got_left, odd_before)
+            spectra(from_left.at[u], *forward, put_halo)
+            a, h = u // heap, heap - 1 - u % heap
+            row, col = spot(h)
+            first = (before // 2 + heap - 1 - h) // heap
+
+            def body(b, carry):
+                whole = (odd_before == 0) | (b * heap + h > before // 2)
+                pairs(
+                    lambda c: halo[c],
+                    lambda c: spec[b, row, col + c],
+                    width, n, *inverse, keep(local + a, a + b + 1, h * width, whole, None, fresh),
+                )
+                return carry
+
+            lax.fori_loop(first, reach - a, body, 0)
+
+        return carry
+
+    lax.fori_loop(0, got, far, 0)
+
+    for stage in stages[window:]:
+        stage()
+    late[...] = ratios(local + reach)
+
+    def copy(source, peer):
+        return pltpu.make_async_remote_copy(
+            src_ref=late,
+            dst_ref=lates.at[source % tiles * groups + source // tiles],
             send_sem=send.at[peer],
-            recv_sem=recv.at[slot],
+            recv_sem=recv.at[source],
             device_id=place(peer),
             device_id_type=MESH,
         )
@@ -397,20 +508,24 @@
         lax.fori_loop(0, others, visit, 0, unroll=others <= 64)
 
     peers(lambda peer: copy(me, peer).start())
-    slots[me] = payload[...]
-
-    def finish(peer):
-        copy(peer, peer).wait_recv()
-        copy(me, peer).wait_send()
-
-    peers(finish)
+    lates[mine] = late[...]
+    columns(lambda other: tile_copy(other, other).wait_recv())
+    columns(lambda other: tile_copy(tile, other).wait_send())
+
+    def sent(k, carry):
+        done = lambda copy: copy.wait_send()
+        each(copy_left, done, k, sent_left, odd_before)
+        each(copy_right, done, k, sent_right, odd_near)
+        return carry
+
+    lax.fori_loop(0, units, sent, 0)
 
     lane = lax.broadcasted_iota(jnp.int32, (TILE, LANES), 1)
     sub = lax.broadcasted_iota(jnp.int32, (TILE, LANES), 0)
     owner = lane % half // span
     total = groups * local
     for g in range(groups):
-        flat = jnp.broadcast_to(slots[g * tiles, local : local + 1], (TILE, LANES))
+        flat = jnp.broadcast_to(slots[g, local : local + 1], (TILE, LANES))
         for v in range(reach):
             w = jnp.sum(jnp.where(lane == v * local + sub, flat, 0.0), axis=1, keepdims=True)
             w = jnp.broadcast_to(w, (TILE, LANES))
@@ -418,9 +533,9 @@
             weight[v, g * local : (g + 1) * local, :] = w[:local]
         blocks = []
         for t in range(tiles):
-            block = slots[g * tiles + t, :local]
+            block = slots[t * groups + g, :local]
             if g < groups - 1:
-                add = slots[(g + 1) * tiles + t, local + 1 :]
+                add = slots[t * groups + g + 1, local + 1 :]
                 block = jnp.concatenate([block[: local - reach], block[local - reach :] + add], axis=0)
             blocks.append(jnp.concatenate([block, jnp.zeros((TILE - local, LANES), jnp.float32)], axis=0))
         for v in range(reach + 1):
@@ -435,6 +550,36 @@
                 value = value * weight[v, g * local : (g + 1) * local, :]
             field[v, g * local : (g + 1) * local, :] = value
 
+    def finish(peer):
+        copy(peer, peer).wait_recv()
+        copy(me, peer).wait_send()
+
+    peers(finish)
+    slot = lax.broadcasted_iota(jnp.int32, (1, LANES), 1) % span // (width // 2)
+    column = lax.broadcasted_iota(jnp.int32, (groups, LANES), 1) % half // span
+    blocks = [lates[pl.ds(t * groups, groups), 0, :] for t in range(tiles)]
+    for v in range(reach):
+        value = jnp.zeros((groups, LANES), jnp.float32)
+        for t in range(tiles):
+            block = blocks[t]
+            if t != v:
+                block = pltpu.roll(block, (t - v) * span % LANES, 1)
+            value = jnp.where(column == t, block, value)
+        for g in range(groups):
+            found = {}
+            for (o, part), section in sorted(cells[g].items()):
+                if o == v:
+                    found.setdefault(section, []).append(part)
+            for section, places in sorted(found.items()):
+                line = value[g : g + 1]
+                if len(found) > 1:
+                    inside = slot == places[0]
+                    for part in places[1:]:
+                        inside = inside | (slot == part)
+                    line = jnp.where(inside, line, 0.0)
+                here = slice(section, section + 1)
+                field[v, here, :] = field[v, here, :] + line * weight[v, here, :]
+
     grid_rows = tiles * rows
     at = lax.broadcasted_iota(jnp.int32, (total, LANES), 1) % half
     across = at % cols
@@ -479,7 +624,12 @@
     width = cols // 2
     units = reach * rows * cols // width
     tab = jnp.asarray(tables(n))
-    sizes = (groups, tiles, local, reach, rows, cols, n, width)
+    heap = units // reach
+    window = 3
+    while window > 1 and late_cells(groups, local, reach, heap, window) is None:
+        window -= 1
+    cells = late_cells(groups, local, reach, heap, window)
+    sizes = (groups, tiles, local, reach, rows, cols, n, width, window, cells)
     hbm = pl.BlockSpec(memory_space=pltpu.HBM)
     vmem = pl.BlockSpec(memory_space=pltpu.VMEM)
     dma = pltpu.SemaphoreType.DMA
@@ -500,9 +650,10 @@
             pltpu.VMEM((units, width, n, n), jnp.bfloat16),
             pltpu.VMEM((local, rows, cols, 2 * part, n), jnp.float32),
             pltpu.VMEM((width, 2 * part, n), jnp.float32),
-            pltpu.VMEM((local + reach, LANES, LANES), jnp.float32),
-            pltpu.VMEM((local + reach + 1, LANES), jnp.float32),
+            pltpu.VMEM((local + reach + 1, LANES, LANES), jnp.float32),
             pltpu.VMEM((groups * tiles, local + reach + 1, LANES), jnp.float32),
+            pltpu.VMEM((1, LANES), jnp.float32),
+            pltpu.VMEM((groups * tiles, 1, LANES), jnp.float32),
             pltpu.VMEM((reach + 1, groups * local, LANES), jnp.float32),
             pltpu.VMEM((reach, groups * local, LANES), jnp.float32),
             dma,
@@ -515,6 +666,11 @@
             dma((groups * tiles,)),
             dma((groups * tiles,)),
             pltpu.SemaphoreType.REGULAR((2,)),
+            dma((2,)),
+            dma((groups // 2,)),
+            dma((groups // 2,)),
+            dma((tiles,)),
+            dma((tiles,)),
         ],
         compiler_params=pltpu.CompilerParams(
             collective_id=0, has_side_effects=True, vmem_limit_bytes=48 << 20

time: 46.9 us -> 47.4 us (1.011)
  Pallas kernels: 44.9 us -> 45.4 us
where the time goes in v3:
time: 47.4 us; the launch traced here: 47.2 us
  Pallas kernels  45.4 us (96%)
  local copies, waits for them, and re-layouts  1.22 us (3%)
  between operations  0.64 us (1%)
    pallas_call x1, Pallas kernels, shards(): pl.pallas_call(functools.partial(kernel, sizes), in_specs=[hbm] * 4, out_...  45.4 us
    unnamed x2, local copies, waits for them, and re-layouts  1.22 us

profile of v3, /device:TPU:0, one launch (start us, length us, event | category | flops | bytes accessed | tf_op | source)
XLA Modules:
  0.0 47.2 jit_solution(11678994161576343854)
XLA Ops:
  0.6 45.4 %align.1 = (f32[2,6,2,8]{3,2,1,0:T(2,128)S(1)}, f32[2,6,3,2,8]{4,3,2,1,0:T(2,128)S(1)}) custom-call(bf16[6,2,8,128,128]{4,3,2,1,0:T(8,128)(2,1)} %patches.1, bf16[784,256]{1,0:T(8,128)(2,1)} %constant.2.clone.tab_in, f32[2,6,2,8]{3,2,1,0:T(2,128)} %nodes_in.1, s32[3,6]{1,0:T(4,128)} %bitcast.1), custom_call_target="tpu_custom_call" | custom-call | tf_op jit(solution)/shard_map/align/pallas_call | solution.py:636
  46.0 0.6 %copy.8 = f32[2,6,2,8]{3,2,1,0:T(2,128)} copy(f32[2,6,2,8]{3,2,1,0:T(2,128)S(1)} %get-tuple-element.4) | data formatting | bytes 1536
  46.6 0.6 %copy.9 = f32[2,6,3,2,8]{4,3,2,1,0:T(2,128)} copy(f32[2,6,3,2,8]{4,3,2,1,0:T(2,128)S(1)} %get-tuple-element.5) | data formatting | bytes 4608

commit v4 on v3

--- a/solution.py
+++ b/solution.py
@@ -141,9 +141,9 @@
 
 def kernel(
     sizes, patches, tab_in, nodes_in, flags_in, moved, shown,
-    tab, x, nodes, flags, from_right, from_left, spec, halo, stats, slots, late, lates, field, weight,
+    tab, x, nodes, flags, from_right, from_left, spec, halo, stats, slots, combs, late, lates, field, weight,
     tab_sem, small_sem, own_sem, left_send, left_recv, right_send, right_recv, send, recv, chain,
-    pair_sem, even_send, even_recv, tile_send, tile_recv,
+    group_send, group_recv, tile_send, tile_recv,
 ):
     groups, tiles, local, reach, rows, cols, n, width, window, cells = sizes
     half = LANES // 2
@@ -154,11 +154,6 @@
     units = reach * heap
     sec = lax.axis_index("sec")
     tile = lax.axis_index("tile")
-    me = sec * tiles + tile
-    count = groups * tiles
-
-    def place(index):
-        return (index // tiles, index % tiles)
 
     lates[...] = jnp.zeros_like(lates)
     barrier = pltpu.get_barrier_semaphore()
@@ -242,8 +237,8 @@
 
     begin = lambda copy: copy.start()
     odd_sec = sec % 2
-    hold_left = 2 * odd_sec
-    hold_right = 2 - hold_left
+    hold_left = 1 * odd_sec
+    hold_right = 1 - hold_left
 
     def launch(k, carry):
         each(copy_left, begin, k, sent_left, odd_before, k < sent_left - hold_left)
@@ -347,44 +342,32 @@
         total = jnp.where(low, pltpu.roll(above, half, 1), above) / area + EPSILON
         return jnp.where(low, above, along) / area / total
 
-    def pair_copy():
+    def group_copy(source, other):
         return pltpu.make_async_remote_copy(
-            src_ref=slots.at[mine],
-            dst_ref=slots.at[mine],
-            send_sem=pair_sem.at[0],
-            recv_sem=pair_sem.at[1],
-            device_id=(sec + 1 - 2 * odd_sec, tile),
+            src_ref=slots.at[source],
+            dst_ref=slots.at[source],
+            send_sem=group_send.at[other],
+            recv_sem=group_recv.at[source],
+            device_id=(other, tile),
             device_id_type=MESH,
         )
 
-    def even_copy(pair, other):
-        both = pl.ds(tile * groups + 2 * pair, 2)
+    def tile_copy(column, other):
         return pltpu.make_async_remote_copy(
-            src_ref=slots.at[both],
-            dst_ref=slots.at[both],
-            send_sem=even_send.at[other],
-            recv_sem=even_recv.at[pair],
-            device_id=(2 * other + odd_sec, tile),
-            device_id_type=MESH,
-        )
-
-    def tile_copy(column, other):
-        whole = pl.ds(column * groups, groups)
-        return pltpu.make_async_remote_copy(
-            src_ref=slots.at[whole],
-            dst_ref=slots.at[whole],
+            src_ref=combs.at[column],
+            dst_ref=combs.at[column],
             send_sem=tile_send.at[other],
             recv_sem=tile_recv.at[column],
             device_id=(sec, other),
             device_id_type=MESH,
         )
 
-    def evens(act):
+    def groups_else(act):
         def visit(d, carry):
-            act((sec // 2 + d) % (groups // 2))
+            act((sec + d) % groups)
             return carry
 
-        lax.fori_loop(1, groups // 2, visit, 0)
+        lax.fori_loop(1, groups, visit, 0)
 
     def columns(act):
         def visit(d, carry):
@@ -396,31 +379,32 @@
     def publish():
         node_copy.wait()
         flag_copy.wait()
-        slots[mine] = jnp.zeros(slots.shape[1:], jnp.float32)
+        slots[sec] = jnp.zeros(slots.shape[1:], jnp.float32)
         for index in range(local + reach):
             at = index if index < local else 2 * local + reach - index
-            slots[mine, at : at + 1] = ratios(index)
+            slots[sec, at : at + 1] = ratios(index)
         for comp in range(2):
             for row in range(rows):
                 at = comp * half + reach * span + row * cols
-                slots[mine, :local, at : at + cols] = nodes[comp, :, row, :]
+                slots[sec, :local, at : at + cols] = nodes[comp, :, row, :]
         for v in range(reach):
-            slots[mine, local : local + 1, v * local : (v + 1) * local] = flags[v : v + 1, :].astype(
+            slots[sec, local : local + 1, v * local : (v + 1) * local] = flags[v : v + 1, :].astype(
                 jnp.float32
             )
-        pair_copy().start()
+        groups_else(lambda other: group_copy(sec, other).start())
         lax.fori_loop(0, units, launch_held, 0)
 
-    def spread_pairs():
-        pair_copy().wait()
-        evens(lambda other: even_copy(sec // 2, other).start())
-
     def spread_columns():
-        evens(lambda other: even_copy(other, other).wait_recv())
-        evens(lambda other: even_copy(sec // 2, other).wait_send())
+        groups_else(lambda other: group_copy(other, other).wait_recv())
+        groups_else(lambda other: group_copy(sec, other).wait_send())
+        for g in range(groups):
+            block = slots[g, :local]
+            if g < groups - 1:
+                add = slots[g + 1, local + 1 :]
+                block = jnp.concatenate([block[: local - reach], block[local - reach :] + add], axis=0)
+            combs[tile, g * local : (g + 1) * local] = block
         columns(lambda other: tile_copy(tile, other).start())
 
-    stages = (publish, spread_pairs, spread_columns)
 
     def put_halo(c, real, imag):
         halo[c, :part] = real
@@ -430,87 +414,95 @@
 
     def far(k, carry):
         fresh = k >= got - window
-        for number, stage in enumerate(stages[:window]):
-            pl.when(k == got - window + number)(stage)
+        pl.when(k == got - window)(publish)
+        if window > 1:
+            pl.when(k == got - 1)(spread_columns)
 
         u = k - odd_sec * got_right
         k = k - (1 - odd_sec) * got_left
 
-        @pl.when((k >= 0) & (k < got_right))
-        def _():
-            each(copy_left, lambda copy: copy.wait_recv(), k, got_right, odd_near)
-            spectra(from_right.at[k], *forward, put_halo)
-            b, h = k // heap, k % heap
-            row, col = spot(h)
-            whole = (odd_near == 0) | (k < got_right - 1)
-
-            def body(a, carry):
-                pairs(
-                    lambda c: spec[local - 1 - a, row, col + c],
-                    lambda c: halo[c],
-                    width, n, *inverse, keep(local - 1 - a, a + b + 1, h * width, None, whole, fresh),
-                )
-                return carry
-
-            lax.fori_loop(0, reach - b, body, 0)
-
-        @pl.when((u >= 0) & (u < got_left))
-        def _():
-            each(copy_right, lambda copy: copy.wait_recv(), u, got_left, odd_before)
-            spectra(from_left.at[u], *forward, put_halo)
-            a, h = u // heap, heap - 1 - u % heap
-            row, col = spot(h)
-            first = (before // 2 + heap - 1 - h) // heap
-
-            def body(b, carry):
-                whole = (odd_before == 0) | (b * heap + h > before // 2)
-                pairs(
-                    lambda c: halo[c],
-                    lambda c: spec[b, row, col + c],
-                    width, n, *inverse, keep(local + a, a + b + 1, h * width, whole, None, fresh),
-                )
-                return carry
-
-            lax.fori_loop(first, reach - a, body, 0)
+        done = lambda copy: copy.wait_recv()
+        each(copy_left, done, k, got_right, odd_near)
+        each(copy_right, done, u, got_left, odd_before)
+        from_next = (k >= 0) & (k < got_right)
+        from_last = (u >= 0) & (u < got_left)
+        next_spot = k % heap
+        last_spot = heap - 1 - u % heap
+        first = (before // 2 + heap - 1 - last_spot) // heap
+
+        for many in range(1, reach + 1):
+
+            @pl.when(from_next & (reach - k // heap == many))
+            def _():
+                spectra(from_right.at[k], *forward, put_halo)
+                row, col = spot(next_spot)
+                whole = (odd_near == 0) | (k < got_right - 1)
+                for a in range(many):
+                    pairs(
+                        lambda c: spec[local - 1 - a, row, col + c],
+                        lambda c: halo[c],
+                        width, n, *inverse,
+                        keep(local - 1 - a, a + reach - many + 1, next_spot * width, None, whole, fresh),
+                    )
+
+            @pl.when(from_last & (reach - u // heap - first == many))
+            def _():
+                spectra(from_left.at[u], *forward, put_halo)
+                row, col = spot(last_spot)
+                a = u // heap
+                for d in range(many):
+                    b = first + d
+                    whole = (odd_before == 0) | (b * heap + last_spot > before // 2)
+                    pairs(
+                        lambda c: halo[c],
+                        lambda c: spec[b, row, col + c],
+                        width, n, *inverse,
+                        keep(local + a, a + b + 1, last_spot * width, whole, None, fresh),
+                    )
 
         return carry
 
     lax.fori_loop(0, got, far, 0)
 
-    for stage in stages[window:]:
-        stage()
+    if window == 1:
+        spread_columns()
     late[...] = ratios(local + reach)
 
-    def copy(source, peer):
+    far_off = min(groups - 1, -(-SWEEPS * reach // local))
+    deltas = sorted(range(-far_off, far_off + 1), key=lambda delta: -abs(delta))
+
+    def late_copy(delta, to):
         return pltpu.make_async_remote_copy(
             src_ref=late,
-            dst_ref=lates.at[source % tiles * groups + source // tiles],
-            send_sem=send.at[peer],
-            recv_sem=recv.at[source],
-            device_id=place(peer),
+            dst_ref=lates.at[mine],
+            send_sem=send.at[delta + far_off],
+            recv_sem=recv.at[delta + far_off],
+            device_id=(sec + delta, to),
             device_id_type=MESH,
         )
 
-    span_of = 2 * min(groups - 1, -(-SWEEPS * reach // local)) + 1
-    others = span_of * tiles
-
-    def peers(act):
-        def visit(d, carry):
-            to = sec + d // tiles - span_of // 2
-            peer = to * tiles + d % tiles
-
-            @pl.when((to >= 0) & (to < groups) & (peer != me))
-            def _():
-                act(peer)
-
-            return carry
-
-        lax.fori_loop(0, others, visit, 0, unroll=others <= 64)
-
-    peers(lambda peer: copy(me, peer).start())
+    def late_sum(delta):
+        several = lates.at[pl.ds(0, tiles if delta else tiles - 1)]
+        return pltpu.make_async_remote_copy(
+            src_ref=several,
+            dst_ref=several,
+            send_sem=send.at[delta + far_off],
+            recv_sem=recv.at[delta + far_off],
+            device_id=(sec, (tile + 1) % tiles),
+            device_id_type=MESH,
+        )
+
+    def peers(sign, act):
+        for delta in deltas:
+            to = sec + sign * delta
+            pl.when((to >= 0) & (to < groups))(functools.partial(act, delta))
+
+    def send_late(delta):
+        for d in range(0 if delta else 1, tiles):
+            late_copy(delta, (tile + d) % tiles).start()
+
+    peers(1, send_late)
     lates[mine] = late[...]
-    columns(lambda other: tile_copy(other, other).wait_recv())
-    columns(lambda other: tile_copy(tile, other).wait_send())
 
     def sent(k, carry):
         done = lambda copy: copy.wait_send()
@@ -522,7 +514,6 @@
 
     lane = lax.broadcasted_iota(jnp.int32, (TILE, LANES), 1)
     sub = lax.broadcasted_iota(jnp.int32, (TILE, LANES), 0)
-    owner = lane % half // span
     total = groups * local
     for g in range(groups):
         flat = jnp.broadcast_to(slots[g, local : local + 1], (TILE, LANES))
@@ -531,30 +522,18 @@
             w = jnp.broadcast_to(w, (TILE, LANES))
             w = jnp.where(g * local + sub + v + 1 < total, w, 0.0)
             weight[v, g * local : (g + 1) * local, :] = w[:local]
-        blocks = []
+    columns(lambda other: tile_copy(other, other).wait_recv())
+    owner = lax.broadcasted_iota(jnp.int32, (total, LANES), 1) % half // span
+    for v in range(reach + 1):
+        value = jnp.zeros((total, LANES), jnp.float32)
         for t in range(tiles):
-            block = slots[t * groups + g, :local]
-            if g < groups - 1:
-                add = slots[t * groups + g + 1, local + 1 :]
-                block = jnp.concatenate([block[: local - reach], block[local - reach :] + add], axis=0)
-            blocks.append(jnp.concatenate([block, jnp.zeros((TILE - local, LANES), jnp.float32)], axis=0))
-        for v in range(reach + 1):
-            value = jnp.zeros((TILE, LANES), jnp.float32)
-            for t in range(tiles):
-                moved_to = blocks[t]
-                if t != v:
-                    moved_to = pltpu.roll(moved_to, (t - v) * span % LANES, 1)
-                value = jnp.where(owner == t, moved_to, value)
-            value = value[:local]
-            if v < reach:
-                value = value * weight[v, g * local : (g + 1) * local, :]
-            field[v, g * local : (g + 1) * local, :] = value
-
-    def finish(peer):
-        copy(peer, peer).wait_recv()
-        copy(me, peer).wait_send()
-
-    peers(finish)
+            block = combs[t]
+            if t != v:
+                block = pltpu.roll(block, (t - v) * span % LANES, 1)
+            value = jnp.where(owner == t, block, value)
+        field[v] = value * weight[v] if v < reach else value
+
+    peers(-1, lambda delta: late_sum(delta).wait_recv())
     slot = lax.broadcasted_iota(jnp.int32, (1, LANES), 1) % span // (width // 2)
     column = lax.broadcasted_iota(jnp.int32, (groups, LANES), 1) % half // span
     blocks = [lates[pl.ds(t * groups, groups), 0, :] for t in range(tiles)]
@@ -614,6 +593,9 @@
                     shown[comp, :, v, row, :] = piece
                 else:
                     moved[comp, :, row, :] = piece
+
+    columns(lambda other: tile_copy(tile, other).wait_send())
+    peers(1, lambda delta: late_sum(delta).wait_send())
 
 
 def shards(patches, pair_flags, nodes):
@@ -651,7 +633,8 @@
             pltpu.VMEM((local, rows, cols, 2 * part, n), jnp.float32),
             pltpu.VMEM((width, 2 * part, n), jnp.float32),
             pltpu.VMEM((local + reach + 1, LANES, LANES), jnp.float32),
-            pltpu.VMEM((groups * tiles, local + reach + 1, LANES), jnp.float32),
+            pltpu.VMEM((groups, local + reach + 1, LANES), jnp.float32),
+            pltpu.VMEM((tiles, groups * local, LANES), jnp.float32),
             pltpu.VMEM((1, LANES), jnp.float32),
             pltpu.VMEM((groups * tiles, 1, LANES), jnp.float32),
             pltpu.VMEM((reach + 1, groups * local, LANES), jnp.float32),
@@ -663,12 +646,11 @@
             dma((units,)),
             dma((units,)),
             dma((units,)),
-            dma((groups * tiles,)),
-            dma((groups * tiles,)),
+            dma((2 * groups,)),
+            dma((2 * groups,)),
             pltpu.SemaphoreType.REGULAR((2,)),
-            dma((2,)),
-            dma((groups // 2,)),
-            dma((groups // 2,)),
+            dma((groups,)),
+            dma((groups,)),
             dma((tiles,)),
             dma((tiles,)),
         ],

time: 47.4 us -> 45.4 us (0.958)
  Pallas kernels: 45.4 us -> 43.4 us
    pallas_call x1, Pallas kernels: 45.4 us -> 43.4 us  [shards(): pl.pallas_call(functools.partial(kernel, sizes), in_specs=[hbm] * 4, out_...]
where the time goes in v4:
time: 45.4 us; the launch traced here: 45.3 us
  Pallas kernels  43.4 us (96%)
  local copies, waits for them, and re-layouts  1.22 us (3%)
  between operations  0.64 us (1%)
    pallas_call x1, Pallas kernels, shards(): pl.pallas_call(functools.partial(kernel, sizes), in_specs=[hbm] * 4, out_...  43.4 us
    unnamed x2, local copies, waits for them, and re-layouts  1.22 us

profile of v4, /device:TPU:0, one launch (start us, length us, event | category | flops | bytes accessed | tf_op | source)
XLA Modules:
  0.0 45.3 jit_solution(7857081149437384342)
XLA Ops:
  0.6 43.4 %align.1 = (f32[2,6,2,8]{3,2,1,0:T(2,128)S(1)}, f32[2,6,3,2,8]{4,3,2,1,0:T(2,128)S(1)}) custom-call(bf16[6,2,8,128,128]{4,3,2,1,0:T(8,128)(2,1)} %patches.1, bf16[784,256]{1,0:T(8,128)(2,1)} %constant.2.clone.tab_in, f32[2,6,2,8]{3,2,1,0:T(2,128)} %nodes_in.1, s32[3,6]{1,0:T(4,128)} %bitcast.1), custom_call_target="tpu_custom_call" | custom-call | tf_op jit(solution)/shard_map/align/pallas_call | solution.py:618
  44.1 0.6 %copy.8 = f32[2,6,2,8]{3,2,1,0:T(2,128)} copy(f32[2,6,2,8]{3,2,1,0:T(2,128)S(1)} %get-tuple-element.4) | data formatting | bytes 1536
  44.7 0.6 %copy.9 = f32[2,6,3,2,8]{4,3,2,1,0:T(2,128)} copy(f32[2,6,3,2,8]{4,3,2,1,0:T(2,128)S(1)} %get-tuple-element.5) | data formatting | bytes 4608

commit v5 on v4

--- a/solution.py
+++ b/solution.py
@@ -140,8 +140,8 @@
 
 
 def kernel(
-    sizes, patches, tab_in, nodes_in, flags_in, moved, shown,
-    tab, x, nodes, flags, from_right, from_left, spec, halo, stats, slots, combs, late, lates, field, weight,
+    sizes, patches, tab_in, nodes_in, flags_in, field, weight,
+    tab, x, nodes, flags, from_right, from_left, spec, halo, stats, slots, combs, late, lates,
     tab_sem, small_sem, own_sem, left_send, left_recv, right_send, right_recv, send, recv, chain,
     group_send, group_recv, tile_send, tile_recv,
 ):
@@ -559,6 +559,17 @@
                 here = slice(section, section + 1)
                 field[v, here, :] = field[v, here, :] + line * weight[v, here, :]
 
+    columns(lambda other: tile_copy(tile, other).wait_send())
+    peers(1, lambda delta: late_sum(delta).wait_send())
+
+
+def relax(sizes, field, weight, moved, shown, final):
+    groups, tiles, local, reach, rows, cols = sizes[:6]
+    half = LANES // 2
+    span = rows * cols
+    total = groups * local
+    sec = lax.axis_index("sec")
+    tile = lax.axis_index("tile")
     grid_rows = tiles * rows
     at = lax.broadcasted_iota(jnp.int32, (total, LANES), 1) % half
     across = at % cols
@@ -581,10 +592,11 @@
             spring = spring + r - pltpu.roll(r, o, 0)
         return u + STEP_SIZE * (plane + spring)
 
-    field[reach] = lax.fori_loop(0, SWEEPS, sweep, field[reach])
+    final[...] = lax.fori_loop(0, SWEEPS, sweep, field[reach])
     back = (LANES - tile * span) % LANES
     for v in range(reach + 1):
-        mine = pltpu.roll(field[v, pl.ds(sec * local, local), :], back, 1)
+        source = field.at[v] if v < reach else final
+        mine = pltpu.roll(source[pl.ds(sec * local, local), :], back, 1)
         for comp in range(2):
             for row in range(rows):
                 at = comp * half + row * cols
@@ -593,9 +605,6 @@
                     shown[comp, :, v, row, :] = piece
                 else:
                     moved[comp, :, row, :] = piece
-
-    columns(lambda other: tile_copy(tile, other).wait_send())
-    peers(1, lambda delta: late_sum(delta).wait_send())
 
 
 def shards(patches, pair_flags, nodes):
@@ -615,13 +624,13 @@
     hbm = pl.BlockSpec(memory_space=pltpu.HBM)
     vmem = pl.BlockSpec(memory_space=pltpu.VMEM)
     dma = pltpu.SemaphoreType.DMA
-    return pl.pallas_call(
+    field, weight = pl.pallas_call(
         functools.partial(kernel, sizes),
         in_specs=[hbm] * 4,
         out_specs=[vmem] * 2,
         out_shape=[
-            jax.ShapeDtypeStruct((2, local, rows, cols), jnp.float32),
-            jax.ShapeDtypeStruct((2, local, reach, rows, cols), jnp.float32),
+            jax.ShapeDtypeStruct((reach + 1, groups * local, LANES), jnp.float32),
+            jax.ShapeDtypeStruct((reach, groups * local, LANES), jnp.float32),
         ],
         scratch_shapes=[
             pltpu.VMEM(tab.shape, jnp.bfloat16),
@@ -637,8 +646,6 @@
             pltpu.VMEM((tiles, groups * local, LANES), jnp.float32),
             pltpu.VMEM((1, LANES), jnp.float32),
             pltpu.VMEM((groups * tiles, 1, LANES), jnp.float32),
-            pltpu.VMEM((reach + 1, groups * local, LANES), jnp.float32),
-            pltpu.VMEM((reach, groups * local, LANES), jnp.float32),
             dma,
             dma((2,)),
             dma((local,)),
@@ -659,6 +666,18 @@
         ),
         name="align",
     )(*[pltpu.with_memory_space_constraint(a, pltpu.HBM) for a in (patches, tab, nodes, pair_flags.T)])
+    return pl.pallas_call(
+        functools.partial(relax, sizes),
+        in_specs=[vmem] * 2,
+        out_specs=[vmem] * 2,
+        out_shape=[
+            jax.ShapeDtypeStruct((2, local, rows, cols), jnp.float32),
+            jax.ShapeDtypeStruct((2, local, reach, rows, cols), jnp.float32),
+        ],
+        scratch_shapes=[pltpu.VMEM((groups * local, LANES), jnp.float32)],
+        compiler_params=pltpu.CompilerParams(vmem_limit_bytes=8 << 20),
+        name="relax",
+    )(field, weight)
 
 
 def solution(mesh):

time: 45.4 us -> 44.8 us (0.987)
  local copies, waits for them, and re-layouts: 1.22 us -> 0 us
  Pallas kernels: 43.4 us -> 44 us
    pallas_call x0 -> x1, Pallas kernels: none -> 1.62 us  [shards(): pl.pallas_call(functools.partial(relax, sizes), in_specs=[vmem] * 2, out_...]
    unnamed x2 -> x0, local copies, waits for them, and re-layouts: 1.22 us -> none
    pallas_call x1, Pallas kernels: 43.4 us -> 42.4 us  [shards(): pl.pallas_call(functools.partial(kernel, sizes), in_specs=[hbm] * 4, out_...]
where the time goes in v5:
time: 44.8 us; the launch traced here: 44.7 us
  Pallas kernels  44 us (98%)
  between operations  0.64 us (1%)
    pallas_call x1, Pallas kernels, shards(): pl.pallas_call(functools.partial(kernel, sizes), in_specs=[hbm] * 4, out_...  42.4 us
    pallas_call x1, Pallas kernels, shards(): pl.pallas_call(functools.partial(relax, sizes), in_specs=[vmem] * 2, out_...  1.62 us

profile of v5, /device:TPU:0, one launch (start us, length us, event | category | flops | bytes accessed | tf_op | source)
XLA Modules:
  0.0 44.7 jit_solution(9519687262456120769)
XLA Ops:
  0.6 42.4 %align.1 = (f32[4,48,128]{2,1,0:T(8,128)S(1)}, f32[3,48,128]{2,1,0:T(8,128)S(1)}) custom-call(bf16[6,2,8,128,128]{4,3,2,1,0:T(8,128)(2,1)} %patches.1, bf16[784,256]{1,0:T(8,128)(2,1)} %constant.2.clone.tab_in, f32[2,6,2,8]{3,2,1,0:T(2,128)} %nodes_in.1, s32[3,6]{1,0:T(4,128)} %bitcast.1), custom_call_target="tpu_custom_call" | custom-call | tf_op jit(solution)/shard_map/align/pallas_call | solution.py:627
  43.1 1.6 %relax.1 = (f32[2,6,2,8]{3,2,1,0:T(2,128)}, f32[2,6,3,2,8]{4,3,2,1,0:T(2,128)}) custom-call(f32[4,48,128]{2,1,0:T(8,128)S(1)} %get-tuple-element.4.field, f32[3,48,128]{2,1,0:T(8,128)S(1)} %get-tuple-element.5.weight), custom_call_target="tpu_custom_call" | custom-call | tf_op jit(solution)/shard_map/relax/pallas_call | solution.py:669

commit v6 on v5

--- a/solution.py
+++ b/solution.py
@@ -430,35 +430,44 @@
         last_spot = heap - 1 - u % heap
         first = (before // 2 + heap - 1 - last_spot) // heap
 
+        end_next = (odd_near == 1) & (k == got_right - 1)
+        end_last = (odd_before == 1) & (u == got_left - 1)
+
+        def next_unit(many, size):
+            spectra(from_right.at[k, pl.ds(0, size)], *forward, put_halo)
+            row, col = spot(next_spot)
+            for a in range(many):
+                pairs(
+                    lambda c: spec[local - 1 - a, row, col + c],
+                    lambda c: halo[c],
+                    size, n, *inverse,
+                    keep(local - 1 - a, a + reach - many + 1, next_spot * width, fresh=fresh),
+                )
+
+        def last_unit(many, size):
+            rest = width - size
+            spectra(from_left.at[u, pl.ds(rest, size)], *forward, put_halo)
+            row, col = spot(last_spot)
+            a = u // heap
+            for d in range(many):
+                b = first + d
+                whole = None
+                if size == width:
+                    whole = (odd_before == 0) | (b * heap + last_spot > before // 2)
+                pairs(
+                    lambda c: halo[c],
+                    lambda c: spec[b, row, col + rest + c],
+                    size, n, *inverse,
+                    keep(local + a, a + b + 1, last_spot * width + rest, whole, None, fresh),
+                )
+
         for many in range(1, reach + 1):
-
-            @pl.when(from_next & (reach - k // heap == many))
-            def _():
-                spectra(from_right.at[k], *forward, put_halo)
-                row, col = spot(next_spot)
-                whole = (odd_near == 0) | (k < got_right - 1)
-                for a in range(many):
-                    pairs(
-                        lambda c: spec[local - 1 - a, row, col + c],
-                        lambda c: halo[c],
-                        width, n, *inverse,
-                        keep(local - 1 - a, a + reach - many + 1, next_spot * width, None, whole, fresh),
-                    )
-
-            @pl.when(from_last & (reach - u // heap - first == many))
-            def _():
-                spectra(from_left.at[u], *forward, put_halo)
-                row, col = spot(last_spot)
-                a = u // heap
-                for d in range(many):
-                    b = first + d
-                    whole = (odd_before == 0) | (b * heap + last_spot > before // 2)
-                    pairs(
-                        lambda c: halo[c],
-                        lambda c: spec[b, row, col + c],
-                        width, n, *inverse,
-                        keep(local + a, a + b + 1, last_spot * width, whole, None, fresh),
-                    )
+            next_many = from_next & (reach - k // heap == many)
+            last_many = from_last & (reach - u // heap - first == many)
+            pl.when(next_many & jnp.logical_not(end_next))(functools.partial(next_unit, many, width))
+            pl.when(next_many & end_next)(functools.partial(next_unit, many, width // 2))
+            pl.when(last_many & jnp.logical_not(end_last))(functools.partial(last_unit, many, width))
+            pl.when(last_many & end_last)(functools.partial(last_unit, many, width // 2))
 
         return carry
 

time: 44.8 us -> 44.6 us (level)
  no operation moved by 1% of the time
where the time goes in v6:
time: 44.6 us; the launch traced here: 44.5 us
  Pallas kernels  43.8 us (98%)
  between operations  0.64 us (1%)
    pallas_call x1, Pallas kernels, shards(): pl.pallas_call(functools.partial(kernel, sizes), in_specs=[hbm] * 4, out_...  42.2 us
    pallas_call x1, Pallas kernels, shards(): pl.pallas_call(functools.partial(relax, sizes), in_specs=[vmem] * 2, out_...  1.62 us

profile of v6, /device:TPU:0, one launch (start us, length us, event | category | flops | bytes accessed | tf_op | source)
XLA Modules:
  0.0 44.5 jit_solution(9545218241599617988)
XLA Ops:
  0.6 42.2 %align.1 = (f32[4,48,128]{2,1,0:T(8,128)S(1)}, f32[3,48,128]{2,1,0:T(8,128)S(1)}) custom-call(bf16[6,2,8,128,128]{4,3,2,1,0:T(8,128)(2,1)} %patches.1, bf16[784,256]{1,0:T(8,128)(2,1)} %constant.2.clone.tab_in, f32[2,6,2,8]{3,2,1,0:T(2,128)} %nodes_in.1, s32[3,6]{1,0:T(4,128)} %bitcast.1), custom_call_target="tpu_custom_call" | custom-call | tf_op jit(solution)/shard_map/align/pallas_call | solution.py:636
  42.9 1.6 %relax.1 = (f32[2,6,2,8]{3,2,1,0:T(2,128)}, f32[2,6,3,2,8]{4,3,2,1,0:T(2,128)}) custom-call(f32[4,48,128]{2,1,0:T(8,128)S(1)} %get-tuple-element.4.field, f32[3,48,128]{2,1,0:T(8,128)S(1)} %get-tuple-element.5.weight), custom_call_target="tpu_custom_call" | custom-call | tf_op jit(solution)/shard_map/relax/pallas_call | solution.py:678
